TPU v7x, 32 devices: a whole 2x2x4 slice. The times are simulated.
32 devices in a mesh: dp: 8 (over z, x), mp: 4 (over y, core).
Axes of the slice: x: 2, y: 2, z: 4, core: 2. Of those that a mesh axis runs over, the one named last changes fastest.
Arguments:
- patches: bfloat16 [32000, 768], P(('dp', 'mp')), may hold values from -6 to 6
- dataset_id: int32 [160], P('dp'), may hold values from 0 to 7
- patch_masks: int32 [8, 200], replicated, may hold values 0 or 1
- mask_tokens: bfloat16 [8, 768], replicated, may hold values from -6 to 6
- key_mask: int32 [160, 200], P('dp'), may hold values from 0 to 1, as said below
- bias_index: int32 [200, 200], replicated, may hold values from 0 to 731
- norm1_gain: float32 [768], replicated, may hold values from 0.5 to 1.5
- norm1_shift: float32 [768], replicated, may hold values from -1.8 to 1.8
- qkv_weight: bfloat16 [768, 3, 768], P(None, None, 'mp'), may hold values from -0.21875 to 0.21875
- query_bias: bfloat16 [768], P('mp'), may hold values from -3 to 3
- value_bias: bfloat16 [768], P('mp'), may hold values from -3 to 3
- bias_table: bfloat16 [732, 12], P(None, 'mp'), may hold values from -5 to 5
- out_weight: bfloat16 [768, 768], P('mp'), may hold values from -1.75 to 1.75
- out_bias: float32 [768], replicated, may hold values from -1.8 to 1.8
- gamma_attn: float32 [768], replicated, may hold values from 0.5 to 2
- norm2_gain: float32 [768], replicated, may hold values from 0.5 to 1.5
- norm2_shift: float32 [768], replicated, may hold values from -1.8 to 1.8
- up_weight: bfloat16 [768, 3072], P(None, 'mp'), may hold values from -0.21875 to 0.21875
- up_bias: bfloat16 [3072], P('mp'), may hold values from -3 to 3
- down_weight: bfloat16 [3072, 768], P('mp'), may hold values from -0.109375 to 0.109375
- down_bias: float32 [768], replicated, may hold values from -1.8 to 1.8
- gamma_mlp: float32 [768], replicated, may hold values from 0.5 to 2
- cotangent: bfloat16 [32000, 768], P(('dp', 'mp')), may hold values from -6 to 6
Outputs:
- output: bfloat16 [32000, 768], P(('dp', 'mp'))
- patch_grad: float32 [32000, 768], P(('dp', 'mp'))
- token_grad: float32 [8, 768], replicated
- norm1_gain_grad: float32 [768], replicated
- norm1_shift_grad: float32 [768], replicated
- qkv_grad: float32 [768, 3, 768], P(None, None, 'mp')
- query_bias_grad: float32 [768], P('mp')
- value_bias_grad: float32 [768], P('mp')
- table_grad: float32 [732, 12], P(None, 'mp')
- out_weight_grad: float32 [768, 768], P('mp')
- out_bias_grad: float32 [768], replicated
- gamma_attn_grad: float32 [768], replicated
- norm2_gain_grad: float32 [768], replicated
- norm2_shift_grad: float32 [768], replicated
- up_weight_grad: float32 [768, 3072], P(None, 'mp')
- up_bias_grad: float32 [3072], P('mp')
- down_weight_grad: float32 [3072, 768], P('mp')
- down_bias_grad: float32 [768], replicated
- gamma_mlp_grad: float32 [768], replicated
Inputs may be any that keep to these rules, and one draw needn't show every extreme that they name: `key_mask`: each row holds ones on a prefix of its positions and zeros after it; the first position is always one.
All inputs are finite; a program needn't handle non-finite values.
Results may differ from a plain program's by a relative error of at most 0.013.
The roundings to bfloat16 on the way count: a program that leaves them out, or rounds other values in their place, can miss the bound.
Values may be sent and summed in bfloat16 or wider, within the bound.
No kernel may reach another device: no remote copies, remote signals or barrier semaphores. Data moves between devices by JAX's collectives and lax.ppermute only.
A program may use at most 192 MiB of HBM per device.

v0:
```python
import jax
import jax.numpy as jnp
from jax import lax
from jax.sharding import PartitionSpec as P

HEAD = 64
SEQ = 200
GROUPS = 8
IMG_BLK = 5


def layer_norm(values, gain, shift):
    mean = jnp.mean(values, axis=-1, keepdims=True)
    centred = values - mean
    spread = jnp.mean(centred * centred, axis=-1, keepdims=True)
    return centred * lax.rsqrt(spread + 1e-06) * gain + shift


def gelu_exact(values):
    return jax.nn.gelu(values, approximate=False)


def product(left, right):
    return jnp.dot(left, right, preferred_element_type=jnp.float32)


def product_first(left, right):
    return lax.dot_general(
        left, right, (((0,), (0,)), ((), ())), preferred_element_type=jnp.float32
    )


def product_last(left, right):
    return lax.dot_general(
        left, right, (((1,), (1,)), ((), ())), preferred_element_type=jnp.float32
    )


def product_cross(left, right):
    return lax.dot_general(
        left, right, (((0,), (1,)), ((), ())), preferred_element_type=jnp.float32
    )


def score_block(queries, keys, bias, key_mask):
    scores = (
        jnp.einsum("bqhe,bkhe->bhqk", queries, keys, preferred_element_type=jnp.float32)
        + bias[None]
    )
    return jnp.where(key_mask[:, None, None, :] > 0, scores, -1e30)


def attention_forward(normed, qkv_all, qbias_all, vbias_all, table_all, masks_here, position_table):
    width = qkv_all.shape[2]
    heads = width // HEAD
    images = masks_here.shape[0]
    scale = HEAD ** (-0.5)
    joint = product(normed, qkv_all.reshape(qkv_all.shape[0], 3 * width))
    shape5 = (images // IMG_BLK, IMG_BLK, SEQ, heads, HEAD)
    queries = (
        ((joint[:, :width] + qbias_all.astype(jnp.float32)) * scale)
        .astype(jnp.bfloat16)
        .reshape(shape5)
    )
    keys = joint[:, width : 2 * width].astype(jnp.bfloat16).reshape(shape5)
    values = (
        (joint[:, 2 * width :] + vbias_all.astype(jnp.float32)).astype(jnp.bfloat16).reshape(shape5)
    )
    bias_flat = product_cross(table_all, position_table)
    bias = bias_flat.reshape(heads, SEQ, SEQ)
    block_masks = masks_here.reshape(images // IMG_BLK, IMG_BLK, SEQ)

    def attend(pieces):
        block_q, block_k, block_v, block_mask = pieces
        scores = score_block(block_q, block_k, bias, block_mask)
        largest = jnp.max(scores, axis=-1, keepdims=True)
        lse = largest + jnp.log(jnp.sum(jnp.exp(scores - largest), axis=-1, keepdims=True))
        probs = jnp.exp(scores - lse).astype(jnp.bfloat16)
        context = jnp.einsum("bhqk,bkhe->bqhe", probs, block_v, preferred_element_type=jnp.float32)
        return (context.astype(jnp.bfloat16), lse)

    context, lse = lax.map(attend, (queries, keys, values, block_masks))
    return (queries, keys, values, block_masks, bias, context.reshape(images * SEQ, width), lse)


def attention_backward(queries, keys, values, block_masks, bias, lse, grad_context, position_table):
    heads = queries.shape[3]
    width = heads * HEAD
    scale = HEAD ** (-0.5)
    grad_blocks = grad_context.reshape(queries.shape)

    def step(total, pieces):
        block_q, block_k, block_v, block_mask, block_lse, block_grad = pieces
        scores = score_block(block_q, block_k, bias, block_mask)
        probs = jnp.exp(scores - block_lse)
        grad_probs = jnp.einsum(
            "bqhe,bkhe->bhqk", block_grad, block_v, preferred_element_type=jnp.float32
        )
        centre = jnp.sum(probs * grad_probs, axis=-1, keepdims=True)
        grad_scores = (probs * (grad_probs - centre)).astype(jnp.bfloat16)
        grad_values = jnp.einsum(
            "bhqk,bqhe->bkhe",
            probs.astype(jnp.bfloat16),
            block_grad,
            preferred_element_type=jnp.float32,
        ).astype(jnp.bfloat16)
        grad_queries = (
            jnp.einsum(
                "bhqk,bkhe->bqhe", grad_scores, block_k, preferred_element_type=jnp.float32
            ).astype(jnp.bfloat16)
            * scale
        )
        grad_keys = jnp.einsum(
            "bhqk,bqhe->bkhe", grad_scores, block_q, preferred_element_type=jnp.float32
        ).astype(jnp.bfloat16)
        total = total + jnp.sum(grad_scores.astype(jnp.float32), axis=0)
        return (total, (grad_queries, grad_keys, grad_values))

    start_total = jnp.zeros((heads, SEQ, SEQ), jnp.float32)
    total, (grad_q, grad_k, grad_v) = lax.scan(
        step, start_total, (queries, keys, values, block_masks, lse, grad_blocks)
    )
    rows = grad_context.shape[0]
    grad_q = grad_q.reshape(rows, width)
    grad_k = grad_k.reshape(rows, width)
    grad_v = grad_v.reshape(rows, width)
    grad_joint = jnp.concatenate([grad_q, grad_k, grad_v], axis=1)
    qbias_local = jnp.sum(grad_q.astype(jnp.float32), axis=0)
    vbias_local = jnp.sum(grad_v.astype(jnp.float32), axis=0)
    total_flat = total.reshape(heads, SEQ * SEQ)
    upper_part = total_flat.astype(jnp.bfloat16)
    lower_part = (total_flat - upper_part.astype(jnp.float32)).astype(jnp.bfloat16)
    stacked = jnp.concatenate([upper_part, lower_part], axis=0)
    table_both = product_cross(position_table, stacked)
    table_local = table_both[:, :heads] + table_both[:, heads:]
    return (grad_joint, qbias_local, vbias_local, table_local)


def local(
    patches,
    dataset_id,
    patch_masks,
    mask_tokens,
    key_mask,
    bias_index,
    norm1_gain,
    norm1_shift,
    qkv_weight,
    query_bias,
    value_bias,
    bias_table,
    out_weight,
    out_bias,
    gamma_attn,
    norm2_gain,
    norm2_shift,
    up_weight,
    up_bias,
    down_weight,
    down_bias,
    gamma_mlp,
    cotangent,
):
    rows = patches.shape[0]
    mp_count = lax.axis_size("mp")
    mp_place = lax.axis_index("mp")
    images = dataset_id.shape[0]
    own_images = images // mp_count
    table_rows = bias_table.shape[0]
    own_ids = lax.dynamic_slice_in_dim(dataset_id, mp_place * own_images, own_images, 0)
    own_choose = (own_ids[:, None] == jnp.arange(GROUPS)[None, :]).astype(jnp.bfloat16)
    own_sel = product(own_choose, patch_masks.astype(jnp.bfloat16))
    selected = own_sel.reshape(rows, 1)
    row_choose = jnp.broadcast_to(own_choose[:, None, :], (own_images, SEQ, GROUPS)).reshape(
        rows, GROUPS
    )
    token_rows = jnp.broadcast_to(
        product(own_choose, mask_tokens)[:, None, :], (own_images, SEQ, mask_tokens.shape[1])
    ).reshape(rows, mask_tokens.shape[1])
    position_table = (bias_index.reshape(SEQ * SEQ, 1) == jnp.arange(table_rows)[None, :]).astype(
        jnp.bfloat16
    )
    start = patches.astype(jnp.float32) * (1.0 - selected) + selected * token_rows
    norm1_value, norm1_back = jax.vjp(layer_norm, start, norm1_gain, norm1_shift)
    normed1 = norm1_value.astype(jnp.bfloat16)
    attn_in = lax.all_gather(normed1, "mp", axis=0, tiled=True)
    qkv_all, qbias_all, vbias_all, table_all, out_all = (
        qkv_weight,
        query_bias,
        value_bias,
        bias_table,
        out_weight,
    )
    queries, keys, values, block_masks, bias, context, lse = attention_forward(
        attn_in, qkv_all, qbias_all, vbias_all, table_all, key_mask, position_table
    )
    out_part = product(context, out_all)
    attn_sum = lax.psum_scatter(out_part, "mp", scatter_dimension=0, tiled=True)
    attn_value = attn_sum + out_bias
    middle = start + gamma_attn * attn_value
    norm2_value, norm2_back = jax.vjp(layer_norm, middle, norm2_gain, norm2_shift)
    normed2 = norm2_value.astype(jnp.bfloat16)
    mlp_in = lax.all_gather(normed2, "mp", axis=0, tiled=True)
    up_all, upb_all, down_all = (up_weight, up_bias, down_weight)
    hidden_pre = product(mlp_in, up_all) + upb_all.astype(jnp.float32)
    hidden_act, gelu_back = jax.vjp(gelu_exact, hidden_pre)
    hidden = hidden_act.astype(jnp.bfloat16)
    down_part = product(hidden, down_all)
    mlp_sum = lax.psum_scatter(
        down_part.astype(jnp.bfloat16), "mp", scatter_dimension=0, tiled=True
    ).astype(jnp.float32)
    mlp_value = mlp_sum + down_bias
    output = (middle + gamma_mlp * mlp_value).astype(jnp.bfloat16)
    grad_out = cotangent.astype(jnp.float32)
    gamma_mlp_part = jnp.sum(grad_out * mlp_value, axis=0)
    grad_mlp = (gamma_mlp * grad_out).astype(jnp.bfloat16)
    down_bias_part = jnp.sum(grad_mlp.astype(jnp.float32), axis=0)
    grad_mlp_all = lax.all_gather(grad_mlp, "mp", axis=0, tiled=True)
    down_grad_local = product_first(hidden, grad_mlp_all)
    grad_hidden = product_last(grad_mlp_all, down_all)
    grad_pre = gelu_back(grad_hidden)[0].astype(jnp.bfloat16)
    up_bias_local = jnp.sum(grad_pre.astype(jnp.float32), axis=0)
    up_grad_local = product_first(mlp_in, grad_pre)
    norm2_part = product_last(grad_pre, up_all)
    grad_normed2 = lax.psum_scatter(norm2_part, "mp", scatter_dimension=0, tiled=True)
    up_grad, up_bias_grad, down_grad = (up_grad_local, up_bias_local, down_grad_local)
    grad_middle_norm, norm2_gain_part, norm2_shift_part = norm2_back(grad_normed2)
    grad_middle = grad_out + grad_middle_norm
    gamma_attn_part = jnp.sum(grad_middle * attn_value, axis=0)
    grad_attn = (gamma_attn * grad_middle).astype(jnp.bfloat16)
    out_bias_part = jnp.sum(grad_attn.astype(jnp.float32), axis=0)
    grad_attn_all = lax.all_gather(grad_attn, "mp", axis=0, tiled=True)
    out_grad_local = product_first(context, grad_attn_all)
    grad_context = product_last(grad_attn_all, out_all).astype(jnp.bfloat16)
    grad_joint, qbias_local, vbias_local, table_local = attention_backward(
        queries, keys, values, block_masks, bias, lse, grad_context, position_table
    )
    width = qkv_all.shape[2]
    model_width = qkv_all.shape[0]
    qkv_grad_local = product_first(attn_in, grad_joint).reshape(model_width, 3, width)
    norm1_part = product_last(grad_joint, qkv_all.reshape(model_width, 3 * width))
    grad_normed1 = lax.psum_scatter(
        norm1_part.astype(jnp.bfloat16), "mp", scatter_dimension=0, tiled=True
    ).astype(jnp.float32)
    qkv_grad, qbias_grad, vbias_grad, table_grad, out_grad = (
        qkv_grad_local,
        qbias_local,
        vbias_local,
        table_local,
        out_grad_local,
    )
    grad_start_norm, norm1_gain_part, norm1_shift_part = norm1_back(grad_normed1)
    grad_start = grad_middle + grad_start_norm
    patch_grad = grad_start * (1.0 - selected)
    token_part = lax.dot_general(
        row_choose.astype(jnp.float32),
        grad_start * selected,
        (((0,), (0,)), ((), ())),
        precision=lax.Precision.HIGHEST,
    )
    qkv_grad, qbias_grad, vbias_grad, table_grad, out_grad, up_grad, up_bias_grad, down_grad = (
        lax.psum(
            (
                qkv_grad,
                qbias_grad,
                vbias_grad,
                table_grad,
                out_grad,
                up_grad,
                up_bias_grad,
                down_grad,
            ),
            "dp",
        )
    )
    (
        token_grad,
        norm1_gain_grad,
        norm1_shift_grad,
        out_bias_grad,
        gamma_attn_grad,
        norm2_gain_grad,
        norm2_shift_grad,
        down_bias_grad,
        gamma_mlp_grad,
    ) = lax.psum(
        (
            token_part,
            norm1_gain_part,
            norm1_shift_part,
            out_bias_part,
            gamma_attn_part,
            norm2_gain_part,
            norm2_shift_part,
            down_bias_part,
            gamma_mlp_part,
        ),
        ("dp", "mp"),
    )
    return (
        output,
        patch_grad,
        token_grad,
        norm1_gain_grad,
        norm1_shift_grad,
        qkv_grad,
        qbias_grad,
        vbias_grad,
        table_grad,
        out_grad,
        out_bias_grad,
        gamma_attn_grad,
        norm2_gain_grad,
        norm2_shift_grad,
        up_grad,
        up_bias_grad,
        down_grad,
        down_bias_grad,
        gamma_mlp_grad,
    )


def solution(mesh):
    return jax.shard_map(
        local,
        mesh=mesh,
        in_specs=(
            P(("dp", "mp"), None),
            P("dp"),
            P(),
            P(),
            P("dp", None),
            P(),
            P(),
            P(),
            P(None, None, "mp"),
            P("mp"),
            P("mp"),
            P(None, "mp"),
            P("mp", None),
            P(),
            P(),
            P(),
            P(),
            P(None, "mp"),
            P("mp"),
            P("mp", None),
            P(),
            P(),
            P(("dp", "mp"), None),
        ),
        out_specs=(
            P(("dp", "mp"), None),
            P(("dp", "mp"), None),
            P(),
            P(),
            P(),
            P(None, None, "mp"),
            P("mp"),
            P("mp"),
            P(None, "mp"),
            P("mp", None),
            P(),
            P(),
            P(),
            P(),
            P(None, "mp"),
            P("mp"),
            P("mp", None),
            P(),
            P(),
        ),
        check_vma=False,
    )
```

profile of v0, /device:TPU:0, one launch (start us, length us, event | category | flops | bytes accessed | tf_op | source)
XLA Modules:
  0.0 1081.7 jit_solution(13086309809975984235)
XLA Ops:
  22.6 18.9 %fusion.61 = f32[3,40000]{1,0:T(4,128)} fusion(bf16[732,3]{0,1:T(4,128)(2,1)S(1)} %copy-done.62, s32[40000]{0:T(1024)S(1)} %eq.35), kind=kOutput, calls=%fused_computation.71 | convolution fusion | flops 204960000 | bytes 644392 | tf_op jit(solution)/shard_map/dot_general | solution.py:40
  44.3 26.1 %all-gather.5.cloned.1.call-done = bf16[4000,768]{1,0:T(8,128)(2,1)} async-done(((bf16[1000,768]{1,0:T(8,128)(2,1)}), bf16[4000,768]{1,0:T(8,128)(2,1)}) %all-gather.5.cloned.1.call-update) | async-done | bytes 6144016 | tf_op jit(solution)/shard_map/all_gather | solution.py:186
  92.3 7.6 reshape.239
  117.7 30.9 %while.31 = (s32[]{:T(128)}, bf16[4,5,200,3,64]{2,4,3,1,0:T(8,128)(2,1)}, f32[4,5,3,200,1]{3,2,1,4,0:T(4,128)}, bf16[4,5,200,3,64]{2,4,3,1,0:T(8,128)(2,1)}, s32...) while((s32[]{:T(128)}, ...), condition=%wide.wide.region_5.6_spmd, body=%wide.wide.region_2.5_spmd.sunk | while | flops 160390000 | bytes 11681225 | solution.py:82
  158.8 7.7 fusion.96
  166.7 97.1 %reduce-scatter.5.cloned.1.call-done = f32[1000,768]{1,0:T(8,128)} async-done(((f32[4000,768]{1,0:T(8,128)}), f32[1000,768]{1,0:T(8,128)}) %reduce-scatter.5.cloned.1.call-update) | async-done | bytes 3072016 | tf_op jit(solution)/shard_map/reduce_scatter | solution.py:198
  277.0 43.4 %all-gather.7.cloned.1.call-done = bf16[4000,768]{1,0:T(8,128)(2,1)} async-done(((bf16[1000,768]{1,0:T(8,128)(2,1)}), bf16[4000,768]{1,0:T(8,128)(2,1)}) %all-gather.7.cloned.1.call-update) | async-done | bytes 6144016 | tf_op jit(solution)/shard_map/all_gather | solution.py:203
  320.4 13.8 %fusion.97 = f32[4000,768]{1,0:T(8,128)} fusion(bf16[4000,768]{1,0:T(8,128)(2,1)} %all-gather.7.cloned.1.call-done, bf16[768,768]{1,0:T(8,128)(2,1)} %param.44), kind=kOutput, calls=%fused_computation.165 | convolution fusion | flops 4718592000 | bytes 19611648 | tf_op jit(solution)/shard_map/dot_general | solution.py:24
  334.2 33.8 %all-gather.9.cloned.1.call-done = bf16[4000,768]{1,0:T(8,128)(2,1)} async-done(((bf16[1000,768]{1,0:T(8,128)(2,1)}), bf16[4000,768]{1,0:T(8,128)(2,1)}) %all-gather.9.cloned.1.call-update) | async-done | bytes 6144016 | tf_op jit(solution)/shard_map/all_gather | solution.py:218
  368.0 36.0 %convert_reduce_fusion.1 = (f32[768]{0:T(1024)}, bf16[4000,768]{1,0:T(8,128)(2,1)S(1)}, f32[4000,768]{1,0:T(8,128)}) fusion(f32[4000,768]{1,0:T(8,128)} %fusion.97, f32[768]{0:T(1024)S(1)} %convert_element_type.138, bf16[4000,768]{1,0:T(8,128)(2,1)} %all-gather.9.cloned.1.call-done, bf16[768,768]{1,0:T(8,128)(2,1)S(1)} %copy-done), kind=kOutput, calls=%fused_computation.74 | convolution fusion | flops 4948990976 | bytes 38049792 | tf_op jit(solution)/shard_map/dot_general | solution.py:34
  406.5 7.9 fusion.98
  414.7 11.1 %multiply_convert_fusion.1 = bf16[4000,768]{1,0:T(8,128)(2,1)S(1)} fusion(f32[4000,768]{1,0:T(8,128)} %get-tuple-element.343, f32[4000,768]{1,0:T(8,128)} %fusion.97, f32[768]{0:T(1024)S(1)} %convert_element_type.138), kind=kLoop, calls=%fused_computation.76 | loop fusion | flops 12288000 | bytes 30723072 | tf_op jit(solution)/shard_map/convert_element_type | solution.py:207
  436.4 75.3 %reduce-scatter.9.cloned.1.call-done = f32[1000,768]{1,0:T(8,128)} async-done(((f32[4000,768]{1,0:T(8,128)}), f32[1000,768]{1,0:T(8,128)}) %reduce-scatter.9.cloned.1.call-update) | async-done | bytes 3072016 | tf_op jit(solution)/shard_map/reduce_scatter | solution.py:225
  514.6 56.9 %reduce-scatter.7.cloned.1.call-done = bf16[1000,768]{1,0:T(8,128)(2,1)} async-done(((bf16[4000,768]{1,0:T(8,128)(2,1)}), bf16[1000,768]{1,0:T(8,128)(2,1)}) %reduce-scatter.7.cloned.1.call-update) | async-done | bytes 1536016 | tf_op jit(solution)/shard_map/reduce_scatter | solution.py:209
  580.2 43.9 %all-gather.11.cloned.1.call-done = bf16[4000,768]{1,0:T(8,128)(2,1)} async-done(((bf16[1000,768]{1,0:T(8,128)(2,1)}), bf16[4000,768]{1,0:T(8,128)(2,1)}) %all-gather.11.cloned.1.call-update) | async-done | bytes 6144016 | tf_op jit(solution)/shard_map/all_gather | solution.py:232
  644.0 85.4 %while.32 = (s32[]{:T(128)}, f32[3,200,200]{1,2,0:T(8,128)}, bf16[4,5,200,3,64]{2,4,3,1,0:T(8,128)(2,1)}, bf16[4,5,200,3,64]{2,4,3,1,0:T(8,128)(2,1)}, bf16[4,5,...) while((s32[]{:T(128)}, f32[3,200,200]{1,2,0:T(8,128)}, ...), condition=%wide.wide.region_16.17_spmd.clone, body=%wide.wide.region_13.16_spmd.clone.sunk | while | flops 392062016 | bytes 36752904 | solution.py:120
  757.6 9.4 convolution_convert_fusion.2
  767.7 10.0 fusion.100
  777.7 10.6 fusion.101
  794.4 7.8 fusion.102
  806.3 23.4 %fusion.57 = f32[732,6]{0,1:T(8,128)S(1)} fusion(s32[40000]{0:T(1024)} %copy-done.36, bf16[3,40000]{1,0:T(4,128)(2,1)S(1)} %get-tuple-element.344, bf16[3,40000]{1,0:T(4,128)(2,1)} %get-tuple-element.345), kind=kOutput, calls=%fused_computation.67 | convolution fusion | flops 381600000 | bytes 657568 | tf_op jit(solution)/shard_map/dot_general | solution.py:40
  829.8 39.7 %all-reduce.1 = (f32[192]{0:T(256)}, f32[192]{0:T(256)}, f32[732,3]{0,1:T(4,128)}, f32[768]{0:T(1024)}) all-reduce(f32[192]{0:T(256)S(1)} %reduce_sum.245, f32[192]{0:T(256)S(1)} %reduce_sum.247, f32[732,3]{0,1:T(4,128)S(1)} %slice_add_fusion.2, f32[768]{0:T(1024)S(1)} %copy-done.55), channel_id=1, replica_groups=mesh['dp'=8,'mp'=4] {'dp'}, use_global_device_ids=true, to_apply=%region_27.28 | all-reduce | flops 3348 | bytes 26784 | tf_op jit(solution)/shard_map/psum | solution.py:262
  888.4 41.2 %all-reduce = (f32[8,768]{1,0:T(8,128)}, f32[768]{0:T(1024)}, f32[768]{0:T(1024)}, f32[768]{0:T(1024)}, f32[768]{0:T(1024)}, /*index=5*/f32[768]{0:T(1024)}, f32[768]{0:T(1024)}, f32[768]{0:T(1024)}, f32[768]{0:T(1024)}) all-reduce(f32[8,768]{1,0:T(8,128)S(1)} %fusion.77, ...), channel_id=1, replica_groups=mesh['dp'=8,'mp'=4] {'dp','mp'}, use_global_device_ids=true, to_apply=%region_20.21 | all-reduce | flops 12288 | bytes 98304 | tf_op jit(solution)/shard_map/psum | solution.py:286
  929.6 138.8 %all-reduce.5.cloned.1.call-done = (f32[768,3,192]{0,2,1:T(8,128)}, f32[192,768]{1,0:T(8,128)}, f32[768,768]{1,0:T(8,128)}, f32[768,768]{1,0:T(8,128)}) async-done(((f32[768,3,192]{0,2,1:T(8,128)}, f32[192,768]{1,0:T(8,128)}, f32[768,768]{1,0:T(8,128)}, f32[768,768]{1,0:T(8,128)}), (f32[768,3,192]{0,2,1:T(8,128)}, f32[192,768]{1,0:T(8,128)}, f32[768,768]{1,0:T(8,128)}, ...) | async-done | bytes 7077904 | tf_op jit(solution)/shard_map/psum | solution.py:262
  (306 shorter events, 306.4 us)
Async XLA Ops:
  7.2 360.8 %copy-start = (bf16[768,768]{1,0:T(8,128)(2,1)S(1)}, bf16[768,768]{1,0:T(8,128)(2,1)}, u32[]{:S(2)}) copy-start(bf16[768,768]{1,0:T(8,128)(2,1)} %param.46) | copy-start | bytes 3538948
  7.2 63.3 %all-gather.5.cloned.1.call-start = ((), (), s32[]{:S(2)}) async-start(), calls=%async_computation.4 | async-start | bytes 7680000 | tf_op jit(solution)/shard_map/all_gather | solution.py:186
  9.0 254.7 %copy-start.31 = (f32[1000]{0:T(1024)}, f32[1000]{0:T(1024)S(1)}, u32[]{:S(2)}) copy-start(f32[1000]{0:T(1024)S(1)} %reshape.234) | copy-start | bytes 12004
  9.0 254.7 %copy-start.34 = (f32[1000]{0:T(1024)}, f32[1000]{0:T(1024)S(1)}, u32[]{:S(2)}) copy-start(f32[1000]{0:T(1024)S(1)} %broadcast_subtract_fusion) | copy-start | bytes 12004
  10.0 253.8 %copy-start.25 = (f32[5,768]{1,0:T(8,128)}, f32[5,768]{1,0:T(8,128)S(1)}, u32[]{:S(2)}) copy-start(f32[5,768]{1,0:T(8,128)S(1)} %fusion.86) | copy-start | bytes 46084
  22.1 241.7 %reduce-scatter.5.cloned.1.call-start = ((), (), s32[]{:S(2)}) async-start(), calls=%async_computation.5 | async-start | bytes 15360000 | tf_op jit(solution)/shard_map/reduce_scatter | solution.py:198
  166.4 97.3 %copy-start.48 = (f32[768]{0:T(1024)S(1)}, f32[768]{0:T(1024)}, u32[]{:S(2)}) copy-start(f32[768]{0:T(1024)} %param.40) | copy-start | bytes 9220
  166.4 97.3 %copy-start.51 = (f32[768]{0:T(1024)S(1)}, f32[768]{0:T(1024)}, u32[]{:S(2)}) copy-start(f32[768]{0:T(1024)} %param.41) | copy-start | bytes 9220
  166.5 153.9 %all-gather.7.cloned.1.call-start = ((), (), s32[]{:S(2)}) async-start(), calls=%async_computation.6 | async-start | bytes 7680000 | tf_op jit(solution)/shard_map/all_gather | solution.py:203
  274.7 93.3 %all-gather.9.cloned.1.call-start = ((), (), s32[]{:S(2)}) async-start(), calls=%async_computation.8 | async-start | bytes 7680000 | tf_op jit(solution)/shard_map/all_gather | solution.py:218
  276.9 234.8 %reduce-scatter.9.cloned.1.call-start = ((), (), s32[]{:S(2)}) async-start(), calls=%async_computation.9 | async-start | bytes 15360000 | tf_op jit(solution)/shard_map/reduce_scatter | solution.py:225
  334.2 72.3 %copy-start.60 = (bf16[768,768]{1,0:T(8,128)(2,1)S(1)}, bf16[768,768]{1,0:T(8,128)(2,1)}, u32[]{:S(2)}) copy-start(bf16[768,768]{1,0:T(8,128)(2,1)} %param.44) | copy-start | bytes 3538948
  414.5 157.1 %reduce-scatter.7.cloned.1.call-start = ((), (), s32[]{:S(2)}) async-start(), calls=%async_computation.7 | async-start | bytes 7680000 | tf_op jit(solution)/shard_map/reduce_scatter | solution.py:209
  436.3 75.4 %copy-start.4 = (f32[1000,768]{1,0:T(8,128)S(1)}, f32[1000,768]{1,0:T(8,128)}, u32[]{:S(2)}) copy-start(f32[1000,768]{1,0:T(8,128)} %multiply_add_fusion) | copy-start | bytes 9216004
  436.3 135.2 %copy-start.50 = (f32[768]{0:T(1024)S(1)}, f32[768]{0:T(1024)}, u32[]{:S(2)}) copy-start(f32[768]{0:T(1024)} %param.47) | copy-start | bytes 9220
  436.3 187.7 %all-gather.11.cloned.1.call-start = ((), (), s32[]{:S(2)}) async-start(), calls=%async_computation.10 | async-start | bytes 7680000 | tf_op jit(solution)/shard_map/all_gather | solution.py:232
  578.4 291.1 %reduce-scatter.11.cloned.1.call-start = ((), (), s32[]{:S(2)}) async-start(), calls=%async_computation.11 | async-start | bytes 7680000 | tf_op jit(solution)/shard_map/reduce_scatter | solution.py:242
  767.0 301.4 %all-reduce.5.cloned.1.call-start = ((), (), s32[]{:S(2)}) async-start(), calls=%async_computation.12 | async-start | bytes 14155776 | tf_op jit(solution)/shard_map/psum | solution.py:262
  806.3 63.2 %copy-start.26 = (f32[5,768]{1,0:T(8,128)S(1)}, f32[5,768]{1,0:T(8,128)}, u32[]{:S(2)}) copy-start(f32[5,768]{1,0:T(8,128)} %copy-done.25) | copy-start | bytes 46084
  806.3 63.2 %copy-start.32 = (f32[1000]{0:T(1024)S(1)}, f32[1000]{0:T(1024)}, u32[]{:S(2)}) copy-start(f32[1000]{0:T(1024)} %copy-done.31) | copy-start | bytes 12004
  806.3 63.2 %copy-start.35 = (f32[1000]{0:T(1024)S(1)}, f32[1000]{0:T(1024)}, u32[]{:S(2)}) copy-start(f32[1000]{0:T(1024)} %copy-done.34) | copy-start | bytes 12004
  806.3 63.2 %copy-start.38 = (f32[1000]{0:T(1024)S(1)}, f32[1000]{0:T(1024)}, u32[]{:S(2)}) copy-start(f32[1000]{0:T(1024)} %copy-done.37) | copy-start | bytes 12004
  806.3 63.2 %copy-start.40 = (f32[1000]{0:T(1024)S(1)}, f32[1000]{0:T(1024)}, u32[]{:S(2)}) copy-start(f32[1000]{0:T(1024)} %copy-done.39) | copy-start | bytes 12004
  806.3 63.2 %copy-start.43 = (f32[768]{0:T(1024)S(1)}, f32[768]{0:T(1024)}, u32[]{:S(2)}) copy-start(f32[768]{0:T(1024)} %param.33) | copy-start | bytes 9220
  (56 other events, 429.3 us)
Sparse Core Ops, SparseCore 0:
  22.2 48.2 all-gather.4
  166.6 97.1 reduce-scatter.4
  274.8 45.5 all-gather.6
  322.4 45.5 all-gather.8
  414.6 97.0 reduce-scatter.8
  514.1 57.3 reduce-scatter.6
  578.5 45.5 all-gather.10
  767.1 57.3 reduce-scatter.10
  830.7 237.6 all-reduce.4
where the time goes:
time: 1090 us; the launch traced here: 1080 us
  waiting for transfers between devices  515 us (47%)
  matrix products  252 us (23%)
  local copies, waits for them, and re-layouts  130 us (12%)
  other arithmetic  87.4 us (8%)
  blocking collectives  80.9 us (7%)
  between operations  14.8 us (1%)
    psum x1, waiting for transfers between devices, local(): lax.psum((qkv_grad, qbias_grad, vbias_grad, table_grad, out_grad, up_grad...  139 us
    reduce_scatter x1, waiting for transfers between devices, local(): attn_sum = lax.psum_scatter(out_part, 'mp', scatter_dimension=0, tiled=True)  97.1 us
    reduce_scatter x1, waiting for transfers between devices, local(): lax.psum_scatter(norm2_part, 'mp', scatter_dimension=0, tiled=True)  75.3 us
    dot_general x4, matrix products, product_last(): lax.dot_general(left, right, (((1,), (1,)), ((), ())), preferred_element_...  59.3 us
    reduce_scatter x1, waiting for transfers between devices, local(): lax.psum_scatter(down_part.astype(jnp.bfloat16), 'mp', scatter_dimension=...  56.9 us
    all_gather x1, waiting for transfers between devices, local(): grad_attn_all = lax.all_gather(grad_attn, 'mp', axis=0, tiled=True)  43.9 us
    all_gather x1, waiting for transfers between devices, local(): mlp_in = lax.all_gather(normed2, 'mp', axis=0, tiled=True)  43.4 us
    dot_general x2, matrix products, product_cross(): lax.dot_general(left, right, (((0,), (1,)), ((), ())), preferred_element_...  42.3 us
  transfers between devices with their start and end apart: 9, of which 8 were waited for; matrix products, arithmetic and copies ran while one was open for 13% of the time, Pallas kernels for 0%

commit v1 on v0

--- a/solution.py
+++ b/solution.py
@@ -1,3 +1,4 @@
+import functools
 import jax
 import jax.numpy as jnp
 from jax import lax
@@ -7,6 +8,24 @@
 SEQ = 200
 GROUPS = 8
 IMG_BLK = 5
+
+
+def link_thing(state, ax_name):
+    b_now = lax.axis_size(ax_name)
+    piece_now, opened, reply = (b_now, lax.axis_index(ax_name), state.shape[0])
+    m_next, left_arr = (state, 1)
+    while left_arr < piece_now:
+        block_now = lax.ppermute(
+            m_next,
+            axis_name=ax_name,
+            perm=[(num, (num - left_arr) % piece_now) for num in range(piece_now)],
+        )
+        m_next = jnp.concatenate([m_next, block_now], axis=0)
+        left_arr = 2 * left_arr
+    return jnp.roll(m_next, opened * reply, 0)
+
+
+finish_the_meshes = functools.partial(link_thing, ax_name="mp")
 
 
 def layer_norm(values, gain, shift):
@@ -200,7 +219,7 @@
     middle = start + gamma_attn * attn_value
     norm2_value, norm2_back = jax.vjp(layer_norm, middle, norm2_gain, norm2_shift)
     normed2 = norm2_value.astype(jnp.bfloat16)
-    mlp_in = lax.all_gather(normed2, "mp", axis=0, tiled=True)
+    mlp_in = finish_the_meshes(normed2)
     up_all, upb_all, down_all = (up_weight, up_bias, down_weight)
     hidden_pre = product(mlp_in, up_all) + upb_all.astype(jnp.float32)
     hidden_act, gelu_back = jax.vjp(gelu_exact, hidden_pre)

time: 1090 us -> 1140 us (1.046)
  waiting for transfers between devices: 515 us -> 550 us
  local copies, waits for them, and re-layouts: 130 us -> 144 us
    ppermute x0 -> x2, waiting for transfers between devices: none -> 113 us  [link_thing(): lax.ppermute(m_next, axis_name=ax_name, perm=[(num, (num - left_arr) % pi...]
    all_gather x1 -> x0, waiting for transfers between devices: 43.4 us -> none  [local(): mlp_in = lax.all_gather(normed2, 'mp', axis=0, tiled=True)]
    all_gather x1, waiting for transfers between devices: 33.8 us -> 0.01 us  [local(): grad_mlp_all = lax.all_gather(grad_mlp, 'mp', axis=0, tiled=True)]
    unnamed x141 -> x151, local copies, waits for them, and re-layouts: 22.3 us -> 33 us
  transfers between devices with their start and end apart: 9 -> 10, of which waited for: 8 -> 8; matrix products, arithmetic and copies ran while one was open for 13% -> 14% of each run, Pallas kernels for 0% -> 0%
where the time goes in v1:
time: 1140 us; the launch traced here: 1130 us
  waiting for transfers between devices  550 us (48%)
  matrix products  249 us (22%)
  local copies, waits for them, and re-layouts  144 us (13%)
  other arithmetic  89.7 us (8%)
  blocking collectives  81.1 us (7%)
  between operations  15.1 us (1%)
    psum x1, waiting for transfers between devices, local(): lax.psum((qkv_grad, qbias_grad, vbias_grad, table_grad, out_grad, up_grad...  139 us
    ppermute x2, waiting for transfers between devices, link_thing(): lax.ppermute(m_next, axis_name=ax_name, perm=[(num, (num - left_arr) % pi...  113 us
    reduce_scatter x1, waiting for transfers between devices, local(): attn_sum = lax.psum_scatter(out_part, 'mp', scatter_dimension=0, tiled=True)  92.7 us
    reduce_scatter x1, waiting for transfers between devices, local(): lax.psum_scatter(norm2_part, 'mp', scatter_dimension=0, tiled=True)  78.8 us
    dot_general x4, matrix products, product_last(): lax.dot_general(left, right, (((1,), (1,)), ((), ())), preferred_element_...  59.3 us
    reduce_scatter x1, waiting for transfers between devices, local(): lax.psum_scatter(down_part.astype(jnp.bfloat16), 'mp', scatter_dimension=...  56.9 us
    all_gather x1, waiting for transfers between devices, local(): grad_attn_all = lax.all_gather(grad_attn, 'mp', axis=0, tiled=True)  43.9 us
    dot_general x2, matrix products, product_cross(): lax.dot_general(left, right, (((0,), (1,)), ((), ())), preferred_element_...  42.3 us
  transfers between devices with their start and end apart: 10, of which 8 were waited for; matrix products, arithmetic and copies ran while one was open for 14% of the time, Pallas kernels for 0%

profile of v1, /device:TPU:0, one launch (start us, length us, event | category | flops | bytes accessed | tf_op | source)
XLA Modules:
  0.0 1132.3 jit_solution(5210485426724552212)
XLA Ops:
  22.6 18.9 %fusion.61 = f32[3,40000]{1,0:T(4,128)} fusion(bf16[732,3]{0,1:T(4,128)(2,1)S(1)} %copy-done.65, s32[40000]{0:T(1024)S(1)} %eq.38), kind=kOutput, calls=%fused_computation.71 | convolution fusion | flops 204960000 | bytes 644392 | tf_op jit(solution)/shard_map/dot_general | solution.py:59
  44.3 26.1 %all-gather.4.cloned.1.call-done = bf16[4000,768]{1,0:T(8,128)(2,1)} async-done(((bf16[1000,768]{1,0:T(8,128)(2,1)}), bf16[4000,768]{1,0:T(8,128)(2,1)}) %all-gather.4.cloned.1.call-update) | async-done | bytes 6144016 | tf_op jit(solution)/shard_map/all_gather | solution.py:205
  92.3 7.4 reshape.239
  117.5 30.9 %while.31 = (s32[]{:T(128)}, bf16[4,5,200,3,64]{2,4,3,1,0:T(8,128)(2,1)}, f32[4,5,3,200,1]{3,2,1,4,0:T(4,128)}, bf16[4,5,200,3,64]{2,4,3,1,0:T(8,128)(2,1)}, s32...) while((s32[]{:T(128)}, ...), condition=%wide.wide.region_5.6_spmd, body=%wide.wide.region_2.5_spmd.sunk | while | flops 160390000 | bytes 11681225 | solution.py:101
  158.6 7.7 fusion.102
  171.0 92.7 %reduce-scatter.5.cloned.1.call-done = f32[1000,768]{1,0:T(8,128)} async-done(((f32[4000,768]{1,0:T(8,128)}), f32[1000,768]{1,0:T(8,128)}) %reduce-scatter.5.cloned.1.call-update) | async-done | bytes 3072016 | tf_op jit(solution)/shard_map/reduce_scatter | solution.py:217
  275.1 48.9 %collective-permute-done = bf16[1000,768]{1,0:T(8,128)(2,1)S(1)} collective-permute-done((bf16[1000,768]{1,0:T(8,128)(2,1)S(1)}, bf16[1000,768]{1,0:T(8,128)(2,1)S(1)}, u32[]{:S(2)}, u32[]{:S(2)}) %collective-permute-start) | collective-permute-done | bytes 1536032 | tf_op jit(solution)/shard_map/ppermute | solution.py:18
  330.4 64.3 %collective-permute-done.1 = bf16[2000,768]{1,0:T(8,128)(2,1)} collective-permute-done((bf16[2000,768]{1,0:T(8,128)(2,1)}, bf16[2000,768]{1,0:T(8,128)(2,1)}, u32[]{:S(2)}, u32[]{:S(2)}) %collective-permute-start.1) | collective-permute-done | bytes 3072032 | tf_op jit(solution)/shard_map/ppermute | solution.py:18
  405.4 10.5 fusion.70
  415.9 35.9 %convert_reduce_fusion.1 = (f32[768]{0:T(1024)}, bf16[4000,768]{1,0:T(8,128)(2,1)S(1)}, f32[4000,768]{1,0:T(8,128)}) fusion(f32[4000,768]{1,0:T(8,128)} %fusion.70, f32[768]{0:T(1024)S(1)} %convert_element_type.138, bf16[4000,768]{1,0:T(8,128)(2,1)} %all-gather.6.cloned.1.call-done, bf16[768,768]{1,0:T(8,128)(2,1)S(1)} %copy-done), kind=kOutput, calls=%fused_computation.74 | convolution fusion | flops 4948990976 | bytes 38049792 | tf_op jit(solution)/shard_map/dot_general | solution.py:53
  454.4 7.9 fusion.103
  462.6 9.7 multiply_convert_fusion.1
  483.0 78.8 %reduce-scatter.9.cloned.1.call-done = f32[1000,768]{1,0:T(8,128)} async-done(((f32[4000,768]{1,0:T(8,128)}), f32[1000,768]{1,0:T(8,128)}) %reduce-scatter.9.cloned.1.call-update) | async-done | bytes 3072016 | tf_op jit(solution)/shard_map/reduce_scatter | solution.py:244
  564.7 56.9 %reduce-scatter.7.cloned.1.call-done = bf16[1000,768]{1,0:T(8,128)(2,1)} async-done(((bf16[4000,768]{1,0:T(8,128)(2,1)}), bf16[1000,768]{1,0:T(8,128)(2,1)}) %reduce-scatter.7.cloned.1.call-update) | async-done | bytes 1536016 | tf_op jit(solution)/shard_map/reduce_scatter | solution.py:228
  630.2 43.9 %all-gather.8.cloned.1.call-done = bf16[4000,768]{1,0:T(8,128)(2,1)} async-done(((bf16[1000,768]{1,0:T(8,128)(2,1)}), bf16[4000,768]{1,0:T(8,128)(2,1)}) %all-gather.8.cloned.1.call-update) | async-done | bytes 6144016 | tf_op jit(solution)/shard_map/all_gather | solution.py:251
  693.8 85.5 %while.32 = (s32[]{:T(128)}, f32[3,200,200]{1,2,0:T(8,128)}, bf16[4,5,200,3,64]{2,4,3,1,0:T(8,128)(2,1)}, bf16[4,5,200,3,64]{2,4,3,1,0:T(8,128)(2,1)}, bf16[4,5,...) while((s32[]{:T(128)}, f32[3,200,200]{1,2,0:T(8,128)}, ...), condition=%wide.wide.region_16.17_spmd.clone, body=%wide.wide.region_13.16_spmd.clone.sunk | while | flops 392062016 | bytes 36752904 | solution.py:139
  807.8 9.4 convolution_convert_fusion.2
  818.0 10.0 fusion.68
  828.0 10.6 fusion.105
  844.7 7.8 fusion.106
  856.6 23.4 %fusion.57 = f32[732,6]{0,1:T(8,128)S(1)} fusion(s32[40000]{0:T(1024)} %copy-done.37, bf16[3,40000]{1,0:T(4,128)(2,1)S(1)} %get-tuple-element.344, bf16[3,40000]{1,0:T(4,128)(2,1)} %get-tuple-element.345), kind=kOutput, calls=%fused_computation.67 | convolution fusion | flops 381600000 | bytes 657568 | tf_op jit(solution)/shard_map/dot_general | solution.py:59
  880.0 39.9 %all-reduce.1 = (f32[192]{0:T(256)}, f32[192]{0:T(256)}, f32[732,3]{0,1:T(4,128)}, f32[768]{0:T(1024)}) all-reduce(f32[192]{0:T(256)S(1)} %reduce_sum.245, f32[192]{0:T(256)S(1)} %reduce_sum.247, f32[732,3]{0,1:T(4,128)S(1)} %slice_add_fusion.2, f32[768]{0:T(1024)S(1)} %copy-done.59), channel_id=1, replica_groups=mesh['dp'=8,'mp'=4] {'dp'}, use_global_device_ids=true, to_apply=%region_27.28 | all-reduce | flops 3348 | bytes 26784 | tf_op jit(solution)/shard_map/psum | solution.py:281
  938.7 41.2 %all-reduce = (f32[8,768]{1,0:T(8,128)}, f32[768]{0:T(1024)}, f32[768]{0:T(1024)}, f32[768]{0:T(1024)}, f32[768]{0:T(1024)}, /*index=5*/f32[768]{0:T(1024)}, f32[768]{0:T(1024)}, f32[768]{0:T(1024)}, f32[768]{0:T(1024)}) all-reduce(f32[8,768]{1,0:T(8,128)S(1)} %fusion.81, ...), channel_id=1, replica_groups=mesh['dp'=8,'mp'=4] {'dp','mp'}, use_global_device_ids=true, to_apply=%region_20.21 | all-reduce | flops 12288 | bytes 98304 | tf_op jit(solution)/shard_map/psum | solution.py:305
  979.9 138.8 %all-reduce.5.cloned.1.call-done = (f32[768,3,192]{0,2,1:T(8,128)}, f32[192,768]{1,0:T(8,128)}, f32[768,768]{1,0:T(8,128)}, f32[768,768]{1,0:T(8,128)}) async-done(((f32[768,3,192]{0,2,1:T(8,128)}, f32[192,768]{1,0:T(8,128)}, f32[768,768]{1,0:T(8,128)}, f32[768,768]{1,0:T(8,128)}), (f32[768,3,192]{0,2,1:T(8,128)}, f32[192,768]{1,0:T(8,128)}, f32[768,768]{1,0:T(8,128)}, ...) | async-done | bytes 7077904 | tf_op jit(solution)/shard_map/psum | solution.py:281
  (319 shorter events, 326.6 us)
Async XLA Ops:
  7.2 408.7 %copy-start = (bf16[768,768]{1,0:T(8,128)(2,1)S(1)}, bf16[768,768]{1,0:T(8,128)(2,1)}, u32[]{:S(2)}) copy-start(bf16[768,768]{1,0:T(8,128)(2,1)} %param.46) | copy-start | bytes 3538948
  7.2 63.3 %all-gather.4.cloned.1.call-start = ((), (), s32[]{:S(2)}) async-start(), calls=%async_computation.4 | async-start | bytes 7680000 | tf_op jit(solution)/shard_map/all_gather | solution.py:205
  9.0 254.6 %copy-start.32 = (f32[1000]{0:T(1024)}, f32[1000]{0:T(1024)S(1)}, u32[]{:S(2)}) copy-start(f32[1000]{0:T(1024)S(1)} %reshape.234) | copy-start | bytes 12004
  9.0 254.6 %copy-start.35 = (f32[1000]{0:T(1024)}, f32[1000]{0:T(1024)S(1)}, u32[]{:S(2)}) copy-start(f32[1000]{0:T(1024)S(1)} %broadcast_subtract_fusion) | copy-start | bytes 12004
  10.0 253.7 %copy-start.26 = (f32[5,768]{1,0:T(8,128)}, f32[5,768]{1,0:T(8,128)S(1)}, u32[]{:S(2)}) copy-start(f32[5,768]{1,0:T(8,128)S(1)} %fusion.90) | copy-start | bytes 46084
  22.1 241.5 %reduce-scatter.5.cloned.1.call-start = ((), (), s32[]{:S(2)}) async-start(), calls=%async_computation.5 | async-start | bytes 15360000 | tf_op jit(solution)/shard_map/reduce_scatter | solution.py:217
  166.3 97.3 %copy-start.50 = (f32[768]{0:T(1024)S(1)}, f32[768]{0:T(1024)}, u32[]{:S(2)}) copy-start(f32[768]{0:T(1024)} %param.40) | copy-start | bytes 9220
  166.3 97.3 %copy-start.53 = (f32[768]{0:T(1024)S(1)}, f32[768]{0:T(1024)}, u32[]{:S(2)}) copy-start(f32[768]{0:T(1024)} %param.41) | copy-start | bytes 9220
  166.4 249.6 %all-gather.6.cloned.1.call-start = ((), (), s32[]{:S(2)}) async-start(), calls=%async_computation.7 | async-start | bytes 7680000 | tf_op jit(solution)/shard_map/all_gather | solution.py:237
  170.5 391.3 %reduce-scatter.9.cloned.1.call-start = ((), (), s32[]{:S(2)}) async-start(), calls=%async_computation.8 | async-start | bytes 15360000 | tf_op jit(solution)/shard_map/reduce_scatter | solution.py:244
  275.1 48.9 %collective-permute-start = (bf16[1000,768]{1,0:T(8,128)(2,1)S(1)}, bf16[1000,768]{1,0:T(8,128)(2,1)S(1)}, u32[]{:S(2)}, u32[]{:S(2)}) collective-permute-start(bf16[1000,768]{1,0:T(8,128)(2,1)S(1)} %get-tuple-element.353), channel_id=1, source_target_pairs={{0,3},{1,0},{2,1},{3,2},{4,7},{5,4},{6,5},{7,6},{8,11},{9,8},{10,9... | collective-permute-start | bytes 4608008 | tf_op jit(solution)/shard_map/ppermute | solution.py:18
  326.1 68.6 %collective-permute-start.1 = (bf16[2000,768]{1,0:T(8,128)(2,1)}, bf16[2000,768]{1,0:T(8,128)(2,1)}, u32[]{:S(2)}, u32[]{:S(2)}) collective-permute-start(bf16[2000,768]{1,0:T(8,128)(2,1)} %pad_maximum_fusion), channel_id=1, source_target_pairs={{0,2},{1,3},{2,0},{3,1},{4,6},{5,7},{6,4},{7,5},{8,10},{9,11},{10,... | collective-permute-start | bytes 9216008 | tf_op jit(solution)/shard_map/ppermute | solution.py:18
  462.3 159.3 %reduce-scatter.7.cloned.1.call-start = ((), (), s32[]{:S(2)}) async-start(), calls=%async_computation.6 | async-start | bytes 7680000 | tf_op jit(solution)/shard_map/reduce_scatter | solution.py:228
  482.9 78.9 %copy-start.4 = (f32[1000,768]{1,0:T(8,128)S(1)}, f32[1000,768]{1,0:T(8,128)}, u32[]{:S(2)}) copy-start(f32[1000,768]{1,0:T(8,128)} %multiply_add_fusion) | copy-start | bytes 9216004
  482.9 138.7 %copy-start.49 = (f32[768]{0:T(1024)S(1)}, f32[768]{0:T(1024)}, u32[]{:S(2)}) copy-start(f32[768]{0:T(1024)} %param.48) | copy-start | bytes 9220
  483.0 138.7 %copy-start.52 = (f32[768]{0:T(1024)S(1)}, f32[768]{0:T(1024)}, u32[]{:S(2)}) copy-start(f32[768]{0:T(1024)} %param.47) | copy-start | bytes 9220
  483.0 191.1 %all-gather.8.cloned.1.call-start = ((), (), s32[]{:S(2)}) async-start(), calls=%async_computation.9 | async-start | bytes 7680000 | tf_op jit(solution)/shard_map/all_gather | solution.py:251
  628.4 291.4 %reduce-scatter.11.cloned.1.call-start = ((), (), s32[]{:S(2)}) async-start(), calls=%async_computation.10 | async-start | bytes 7680000 | tf_op jit(solution)/shard_map/reduce_scatter | solution.py:261
  817.3 301.4 %all-reduce.5.cloned.1.call-start = ((), (), s32[]{:S(2)}) async-start(), calls=%async_computation.11 | async-start | bytes 14155776 | tf_op jit(solution)/shard_map/psum | solution.py:281
  856.5 63.3 %copy-start.33 = (f32[1000]{0:T(1024)S(1)}, f32[1000]{0:T(1024)}, u32[]{:S(2)}) copy-start(f32[1000]{0:T(1024)} %copy-done.32) | copy-start | bytes 12004
  856.5 63.3 %copy-start.36 = (f32[1000]{0:T(1024)S(1)}, f32[1000]{0:T(1024)}, u32[]{:S(2)}) copy-start(f32[1000]{0:T(1024)} %copy-done.35) | copy-start | bytes 12004
  856.6 63.3 %copy-start.39 = (f32[1000]{0:T(1024)S(1)}, f32[1000]{0:T(1024)}, u32[]{:S(2)}) copy-start(f32[1000]{0:T(1024)} %copy-done.38) | copy-start | bytes 12004
  856.6 63.3 %copy-start.41 = (f32[1000]{0:T(1024)S(1)}, f32[1000]{0:T(1024)}, u32[]{:S(2)}) copy-start(f32[1000]{0:T(1024)} %copy-done.40) | copy-start | bytes 12004
  856.6 63.3 %copy-start.44 = (f32[768]{0:T(1024)S(1)}, f32[768]{0:T(1024)}, u32[]{:S(2)}) copy-start(f32[768]{0:T(1024)} %param.33) | copy-start | bytes 9220
  (60 other events, 610.5 us)
Sparse Core Ops, SparseCore 0:
  22.2 48.2 all-gather.3
  166.5 97.1 reduce-scatter.4
  265.8 61.6 all-gather.5
  462.5 99.2 reduce-scatter.8
  564.2 57.3 reduce-scatter.6
  628.5 45.5 all-gather.7
  817.4 57.3 reduce-scatter.10
  881.0 237.6 all-reduce.4
